TPU v7x, 32 devices: a whole 2x2x4 slice. The times are simulated.
32 devices in a mesh: wide: 16 (over z, y, x), narrow: 2 (over core).
Axes of the slice: x: 2, y: 2, z: 4, core: 2. Of those that a mesh axis runs over, the one named last changes fastest.
Arguments:
- pool_tokens: bfloat16 [12288, 2048], P(('wide', 'narrow')), may hold values from -6 to 6
- cotangent: bfloat16 [24576, 2048], P(('wide', 'narrow')), may hold values from -6 to 6
- slot_weights: bfloat16 [32, 3, 2048, 512], P(('wide', 'narrow')), may hold values from -6 to 6
- row_index: int32 [32, 768], P(('wide', 'narrow')), may hold values from 0 to 383
- route_weight: float32 [32, 768], P(('wide', 'narrow')), may hold values from 0.05 to 1
- slot_expert: int32 [32, 1], replicated, may hold values from 0 to 7
- next_expert: int32 [32, 1], replicated, may hold values from 0 to 7
- master: float32 [8, 3, 2048, 512], P(None, None, ('wide', 'narrow')), may hold values from -6 to 6
- moment_m: float32 [8, 3, 2048, 512], P(None, None, ('wide', 'narrow')), may hold values from -4 to 4
- moment_v: float32 [8, 3, 2048, 512], P(None, None, ('wide', 'narrow')), may hold values from 0.05 to 1
Outputs:
- token_grads: bfloat16 [12288, 2048], P(('wide', 'narrow'))
- master_next: float32 [8, 3, 2048, 512], P(None, None, ('wide', 'narrow'))
- moment_m_next: float32 [8, 3, 2048, 512], P(None, None, ('wide', 'narrow'))
- moment_v_next: float32 [8, 3, 2048, 512], P(None, None, ('wide', 'narrow'))
- next_weights: bfloat16 [32, 3, 2048, 512], P(('wide', 'narrow'))
Inputs may be any that keep to these rules, and one draw needn't show every extreme that they name: `slot_expert`: every one of the 8 experts is held by at least one slot; counts are uneven. `next_expert`: every one of the 8 experts is held by at least one slot; counts are uneven. `row_index`: indices into the pool of the slot's own device; a token may appear more than once.
All inputs are finite; a program needn't handle non-finite values.
Results may differ from a plain program's by a relative error of at most 0.0065.
Values may be sent and summed in bfloat16 or wider, within the bound.
A program may use at most 128 MiB of HBM per device.

v0:
```python
import jax
import jax.numpy as jnp
from jax import lax
from jax.sharding import PartitionSpec as P

EXPERTS = 8


def inner(left, right):
    return lax.dot_general(
        left, right, (((0,), (0,)), ((), ())), preferred_element_type=jnp.float32
    )


def against(left, right):
    return lax.dot_general(
        left, right, (((1,), (1,)), ((), ())), preferred_element_type=jnp.float32
    )


def slot_pass(rows, cotangent, weights, route):
    scale_in = weights.shape[1] ** (-0.5)
    scale_out = weights.shape[2] ** (-0.5)
    gate = jnp.dot(rows, weights[0], preferred_element_type=jnp.float32) * scale_in
    upper = jnp.dot(rows, weights[1], preferred_element_type=jnp.float32) * scale_in
    sigma = jax.nn.sigmoid(gate)
    active = gate * sigma
    hidden = (active * upper).astype(jnp.bfloat16)
    scaled = (route[:, None] * cotangent.astype(jnp.float32)).astype(jnp.bfloat16)
    back = jnp.dot(scaled, weights[2], preferred_element_type=jnp.float32) * scale_out
    d_gate = (back * upper * sigma * (1.0 + gate * (1.0 - sigma))).astype(jnp.bfloat16)
    d_up = (back * active).astype(jnp.bfloat16)
    grads = jnp.stack(
        [
            inner(rows, d_gate) * scale_in,
            inner(rows, d_up) * scale_in,
            inner(scaled, hidden) * scale_out,
        ]
    )
    inputs = (against(d_gate, weights[0]) + against(d_up, weights[1])) * scale_in
    return (grads, inputs)


def adam_step(grad, master, moment_m, moment_v):
    first = 0.9 * moment_m + 0.1 * grad
    second = 0.95 * moment_v + 0.05 * grad * grad
    fresh = master - 0.05 * (first / (jnp.sqrt(second) + 1e-08) + 0.1 * master)
    return (fresh, first, second)


def local(
    pool_tokens,
    cotangent,
    slot_weights,
    row_index,
    route_weight,
    slot_expert,
    next_expert,
    master,
    moment_m,
    moment_v,
):
    picked = row_index[0]
    rows = jnp.take(pool_tokens, picked, axis=0)
    grads, inputs = slot_pass(rows, cotangent, slot_weights[0], route_weight[0])
    token_grads = (
        jnp.zeros(pool_tokens.shape, jnp.float32).at[picked].add(inputs).astype(jnp.bfloat16)
    )
    wide_count = lax.axis_size("wide")
    narrow_count = lax.axis_size("narrow")
    members = wide_count * narrow_count
    parts, width, hidden_units = grads.shape
    block = width // members
    received = lax.all_to_all(grads, ("wide", "narrow"), split_axis=1, concat_axis=0, tiled=True)
    received = received.reshape(members, parts, block, hidden_units)
    owners = (slot_expert[:, 0][None, :] == jnp.arange(EXPERTS, dtype=jnp.int32)[:, None]).astype(
        jnp.float32
    )
    summed = jnp.einsum("es,skrh->ekrh", owners, received, precision=lax.Precision.HIGHEST)
    fresh, first, second = adam_step(summed, master, moment_m, moment_v)
    reordered = jnp.transpose(fresh.astype(jnp.bfloat16), (1, 0, 2, 3))
    outgoing = jnp.take(reordered, next_expert[:, 0], axis=1)
    arrived = lax.all_to_all(outgoing, ("wide", "narrow"), split_axis=1, concat_axis=2, tiled=True)
    next_weights = arrived.reshape(1, parts, width, hidden_units)
    return (token_grads, fresh, first, second, next_weights)


def solution(mesh):
    in_specs = (
        P(("wide", "narrow"), None),
        P(("wide", "narrow"), None),
        P(("wide", "narrow"), None, None, None),
        P(("wide", "narrow"), None),
        P(("wide", "narrow"), None),
        P(),
        P(),
        P(None, None, ("wide", "narrow"), None),
        P(None, None, ("wide", "narrow"), None),
        P(None, None, ("wide", "narrow"), None),
    )
    out_specs = (
        P(("wide", "narrow"), None),
        P(None, None, ("wide", "narrow"), None),
        P(None, None, ("wide", "narrow"), None),
        P(None, None, ("wide", "narrow"), None),
        P(("wide", "narrow"), None, None, None),
    )
    return jax.shard_map(local, mesh=mesh, in_specs=in_specs, out_specs=out_specs, check_vma=False)
```

profile of v0, /device:TPU:0, one launch (start us, length us, event | category | flops | bytes accessed | tf_op | source)
XLA Modules:
  0.0 623.8 jit_solution(776716893748135336)
XLA Ops:
  2.2 4.2 gather_fusion
  6.4 5.7 fusion.32
  12.1 4.6 fusion.29
  16.7 5.9 multiply_convert_fusion.2
  22.7 2.2 multiply_bitcast_fusion
  24.9 2.0 multiply_bitcast_fusion.1
  26.9 2.0 multiply_bitcast_fusion.2
  28.9 1.9 pad_maximum_fusion
  30.8 25.5 %copy.44 = f32[3,2048,512]{2,0,1:T(4,128)} copy(f32[3,2048,512]{2,1,0:T(8,128)S(1)} %pad_maximum_fusion) | data formatting | bytes 25165824 | tf_op jit(solution)/shard_map/stack | solution.py:33
  56.3 7.5 %all-to-all-start = ((f32[3,2048,512]{2,0,1:T(4,128)}), f32[3,2048,512]{2,0,1:T(4,128)}, u32[]{:S(2)}, u32[]{:S(2)}) async-start(f32[3,2048,512]{2,0,1:T(4,128)} %copy.44), calls=%async_computation | async-start | bytes 33554432 | tf_op jit(solution)/shard_map/all_to_all | solution.py:74
  63.9 372.5 %all-to-all-done = f32[3,2048,512]{2,0,1:T(4,128)} async-done(((f32[3,2048,512]{2,0,1:T(4,128)}), f32[3,2048,512]{2,0,1:T(4,128)}, u32[]{:S(2)}, u32[]{:S(2)}) %all-to-all-start) | async-done | bytes 12582944 | tf_op jit(solution)/shard_map/all_to_all | solution.py:74
  436.4 26.7 %convert_bitcast_fusion = (bf16[3,8,64,512]{3,1,2,0:T(8,128)(2,1)S(1)}, f32[8,3,64,512]{3,0,2,1:T(8,128)}, f32[8,3,64,512]{3,0,2,1:T(8,128)}, f32[8,3,64,512]{3,0,2,1:T(8,128)}) fusion(f32[8,3,64,512]{3,2,1,0:T(8,128)} %param.17, f32[8,3,64,512]{3,2,1,0:T(8,128)} %param.19, f32[8,3,64,512]{3,2,1,0:T(8,128)} %param.18, f32[3,32,64,512]{3,0,2,1:T(4,128)} %bitcast.10, ...), kind=kOutput, calls=%fused_computation.38 | convolution fusion | flops 313000192 | bytes 33030272 | tf_op jit(solution)/shard_map/es,skrh->ekrh/dot_general | solution.py:79
  463.6 3.7 gather_fusion.1
  467.2 6.1 select_bitcast_fusion
  473.3 3.8 all-to-all-start.1
  477.1 6.1 fusion.9
  483.3 6.0 fusion.13
  489.3 18.8 %scatter_custom_fusion = f32[384,2048]{1,0:T(8,128)} fusion(s32[768]{0:T(1024)S(1)} %fusion.38, f32[768,2048]{1,0:T(8,128)} %fusion.9, f32[768,2048]{1,0:T(8,128)} %fusion.13, f32[]{:T(128)} %constant.13.clone.1, f32[]{:T(128)} %constant.15.clone.1), kind=kCustom, calls=%fused_computation.8 | custom fusion | flops 4718592 | bytes 15728648 | tf_op jit(solution)/shard_map/scatter-add | solution.py:67
  508.1 3.4 convert_element_type.26
  511.5 3.5 copy.52
  515.0 3.5 copy.53
  518.5 3.5 copy.54
  522.0 94.9 %all-to-all-done.1 = bf16[3,32,64,512]{3,2,0,1:T(8,128)(2,1)} async-done(((bf16[3,32,64,512]{3,2,0,1:T(8,128)(2,1)}), bf16[3,32,64,512]{3,2,0,1:T(8,128)(2,1)}, u32[]{:S(2)}, u32[]{:S(2)}) %all-to-all-start.1) | async-done | bytes 6291488 | tf_op jit(solution)/shard_map/all_to_all | solution.py:83
  616.9 6.4 %copy.51 = bf16[3,32,64,512]{3,2,1,0:T(8,128)(2,1)} copy(bf16[3,32,64,512]{3,2,0,1:T(8,128)(2,1)} %all-to-all-done.1) | data formatting | bytes 12582912 | tf_op jit(solution)/shard_map/all_to_all | solution.py:83
  (35 shorter events, 2.1 us)
Async XLA Ops:
  0.6 1.6 copy-start
  6.4 5.7 copy-start.5
  12.1 4.6 copy-start.7
  16.7 6.0 copy-start.9
  16.7 6.0 copy-start.11
  16.7 6.0 copy-start.12
  22.7 2.2 copy-start.6
  56.3 7.5 %copy-start.10 = (s32[32,1]{0,1:T(1,128)S(1)}, s32[32,1]{0,1:T(1,128)}, u32[]{:S(2)}) copy-start(s32[32,1]{0,1:T(1,128)} %param.16) | copy-start | bytes 388
  56.3 380.1 %copy-start.8 = (s32[32,1]{0,1:T(1,128)S(1)}, s32[32,1]{0,1:T(1,128)}, u32[]{:S(2)}) copy-start(s32[32,1]{0,1:T(1,128)} %param.15) | copy-start | bytes 388
  56.3 380.1 %all-to-all-start = ((f32[3,2048,512]{2,0,1:T(4,128)}), f32[3,2048,512]{2,0,1:T(4,128)}, u32[]{:S(2)}, u32[]{:S(2)}) async-start(f32[3,2048,512]{2,0,1:T(4,128)} %copy.44), calls=%async_computation | async-start | bytes 33554432 | tf_op jit(solution)/shard_map/all_to_all | solution.py:74
  473.3 143.6 %all-to-all-start.1 = ((bf16[3,32,64,512]{3,2,0,1:T(8,128)(2,1)}), bf16[3,32,64,512]{3,2,0,1:T(8,128)(2,1)}, u32[]{:S(2)}, u32[]{:S(2)}) async-start(bf16[3,32,64,512]{3,2,0,1:T(8,128)(2,1)} %select_bitcast_fusion), calls=%async_computation.1 | async-start | bytes 12582912 | tf_op jit(solution)/shard_map/all_to_all | solution.py:83
  508.1 3.4 copy-start.4
  511.5 3.5 copy-start.3
  515.0 3.5 copy-start.2
  616.9 6.4 %copy-start.1 = (bf16[384,2048]{1,0:T(8,128)(2,1)S(1)}, bf16[384,2048]{1,0:T(8,128)(2,1)}, u32[]{:S(2)}) copy-start(bf16[384,2048]{1,0:T(8,128)(2,1)} %param.10) | copy-start | bytes 4718596
where the time goes:
time: 632 us; the launch traced here: 624 us
  waiting for transfers between devices  467 us (74%)
  matrix products  61.1 us (10%)
  local copies, waits for them, and re-layouts  50.9 us (8%)
  other arithmetic  31.8 us (5%)
  starting transfers between devices  11.3 us (2%)
    all_to_all x1, waiting for transfers between devices, local(): lax.all_to_all(grads, ('wide', 'narrow'), split_axis=1, concat_axis=0, ti...  373 us
    all_to_all x1, waiting for transfers between devices, local(): lax.all_to_all(outgoing, ('wide', 'narrow'), split_axis=1, concat_axis=2,...  94.9 us
    dot_general x1, matrix products, local(): jnp.einsum('es,skrh->ekrh', owners, received, precision=lax.Precision.HIG...  26.7 us
    another operation x1, local copies, waits for them, and re-layouts, slot_pass(): jnp.stack([inner(rows, d_gate) * scale_in, inner(rows, d_up) * scale_in,...  25.5 us
    scatter-add x1, other arithmetic, local(): jnp.zeros(pool_tokens.shape, jnp.float32).at[picked].add(inputs)  18.8 us
  transfers between devices with their start and end apart: 2, of which 2 were waited for; matrix products, arithmetic and copies ran while one was open for 7% of the time, Pallas kernels for 0%

commit v1 on v0

--- a/solution.py
+++ b/solution.py
@@ -80,7 +80,15 @@
     fresh, first, second = adam_step(summed, master, moment_m, moment_v)
     reordered = jnp.transpose(fresh.astype(jnp.bfloat16), (1, 0, 2, 3))
     outgoing = jnp.take(reordered, next_expert[:, 0], axis=1)
-    arrived = lax.all_to_all(outgoing, ("wide", "narrow"), split_axis=1, concat_axis=2, tiled=True)
+    arrived = jnp.concatenate(
+        lax.all_to_all(
+            jnp.stack(jnp.split(outgoing, lax.axis_size(("wide", "narrow")), 1), 0),
+            split_axis=0,
+            concat_axis=0,
+            axis_name=("wide", "narrow"),
+        ),
+        axis=2,
+    )
     next_weights = arrived.reshape(1, parts, width, hidden_units)
     return (token_grads, fresh, first, second, next_weights)
 

time: 632 us -> 653 us (1.033)
  local copies, waits for them, and re-layouts: 50.9 us -> 75 us
    unnamed x29 -> x58, local copies, waits for them, and re-layouts: 10.5 us -> 33.9 us
where the time goes in v1:
time: 653 us; the launch traced here: 644 us
  waiting for transfers between devices  465 us (71%)
  local copies, waits for them, and re-layouts  75 us (11%)
  matrix products  61.3 us (9%)
  other arithmetic  29.8 us (5%)
  starting transfers between devices  11.1 us (2%)
    all_to_all x1, waiting for transfers between devices, local(): lax.all_to_all(grads, ('wide', 'narrow'), split_axis=1, concat_axis=0, ti...  373 us
    all_to_all x1, waiting for transfers between devices, local(): lax.all_to_all(jnp.stack(jnp.split(outgoing, lax.axis_size(('wide', 'narr...  92.9 us
    unnamed x58, local copies, waits for them, and re-layouts  33.9 us
    dot_general x1, matrix products, local(): jnp.einsum('es,skrh->ekrh', owners, received, precision=lax.Precision.HIG...  26.9 us
    another operation x1, local copies, waits for them, and re-layouts, slot_pass(): jnp.stack([inner(rows, d_gate) * scale_in, inner(rows, d_up) * scale_in,...  25.5 us
    scatter-add x1, other arithmetic, local(): jnp.zeros(pool_tokens.shape, jnp.float32).at[picked].add(inputs)  18.8 us
  transfers between devices with their start and end apart: 2, of which 2 were waited for; matrix products, arithmetic and copies ran while one was open for 7% of the time, Pallas kernels for 0%

profile of v1, /device:TPU:0, one launch (start us, length us, event | category | flops | bytes accessed | tf_op | source)
XLA Modules:
  0.0 643.9 jit_solution(6053165971065901674)
XLA Ops:
  2.9 4.2 gather_fusion
  7.1 5.7 fusion.32
  12.8 4.6 fusion.29
  17.4 5.9 multiply_convert_fusion.2
  23.4 2.2 multiply_bitcast_fusion
  25.6 2.0 multiply_bitcast_fusion.1
  27.6 2.0 multiply_bitcast_fusion.2
  29.6 1.9 pad_maximum_fusion
  31.5 25.5 %copy.75 = f32[3,2048,512]{2,0,1:T(4,128)} copy(f32[3,2048,512]{2,1,0:T(8,128)S(1)} %pad_maximum_fusion) | data formatting | bytes 25165824 | tf_op jit(solution)/shard_map/stack | solution.py:33
  57.0 7.5 %all-to-all-start = ((f32[3,2048,512]{2,0,1:T(4,128)}), f32[3,2048,512]{2,0,1:T(4,128)}, u32[]{:S(2)}, u32[]{:S(2)}) async-start(f32[3,2048,512]{2,0,1:T(4,128)} %copy.75), calls=%async_computation | async-start | bytes 33554432 | tf_op jit(solution)/shard_map/all_to_all | solution.py:74
  64.5 372.6 %all-to-all-done = f32[3,2048,512]{2,0,1:T(4,128)} async-done(((f32[3,2048,512]{2,0,1:T(4,128)}), f32[3,2048,512]{2,0,1:T(4,128)}, u32[]{:S(2)}, u32[]{:S(2)}) %all-to-all-start) | async-done | bytes 12582944 | tf_op jit(solution)/shard_map/all_to_all | solution.py:74
  437.1 26.9 %convert_bitcast_fusion = (bf16[3,8,64,512]{3,1,2,0:T(8,128)(2,1)S(1)}, f32[8,3,64,512]{3,0,2,1:T(8,128)}, f32[8,3,64,512]{3,0,2,1:T(8,128)}, f32[8,3,64,512]{3,0,2,1:T(8,128)}) fusion(f32[8,3,64,512]{3,2,1,0:T(8,128)} %param.17, f32[8,3,64,512]{3,2,1,0:T(8,128)} %param.19, f32[8,3,64,512]{3,2,1,0:T(8,128)} %param.18, f32[3,32,64,512]{3,0,2,1:T(4,128)} %bitcast.10, ...), kind=kOutput, calls=%fused_computation.38 | convolution fusion | flops 313000192 | bytes 33030272 | tf_op jit(solution)/shard_map/es,skrh->ekrh/dot_general | solution.py:79
  464.4 3.7 gather_fusion.1
  468.1 3.4 select_bitcast_fusion
  493.6 3.6 all-to-all-start.1
  497.2 6.1 fusion.9
  503.4 6.0 fusion.13
  509.4 18.8 %scatter_custom_fusion = f32[384,2048]{1,0:T(8,128)} fusion(s32[768]{0:T(1024)S(1)} %fusion.70, f32[768,2048]{1,0:T(8,128)} %fusion.9, f32[768,2048]{1,0:T(8,128)} %fusion.13, f32[]{:T(128)} %constant.13.clone.1, f32[]{:T(128)} %constant.15.clone.1), kind=kCustom, calls=%fused_computation.8 | custom fusion | flops 4718592 | bytes 15728648 | tf_op jit(solution)/shard_map/scatter-add | solution.py:67
  528.2 3.4 convert_element_type.26
  531.6 5.5 copy.83
  537.2 3.5 copy.84
  540.7 3.5 copy.85
  544.1 92.9 %all-to-all-done.1 = bf16[32,3,1,64,512]{4,3,1,2,0:T(8,128)(2,1)} async-done(((bf16[32,3,1,64,512]{4,3,1,2,0:T(8,128)(2,1)}), bf16[32,3,1,64,512]{4,3,1,2,0:T(8,128)(2,1)}, u32[]{:S(2)}, u32[]{:S(2)}) %all-to-all-start.1) | async-done | bytes 6291488 | tf_op jit(solution)/shard_map/all_to_all | solution.py:84
  637.0 6.4 copy.82
  (64 shorter events, 24.9 us)
Async XLA Ops:
  0.6 2.2 copy-start
  7.1 5.7 copy-start.4
  12.8 4.6 copy-start.6
  17.4 6.0 copy-start.8
  17.4 6.0 copy-start.10
  17.4 6.0 copy-start.11
  23.4 2.2 copy-start.5
  57.0 7.5 %copy-start.9 = (s32[32,1]{0,1:T(1,128)S(1)}, s32[32,1]{0,1:T(1,128)}, u32[]{:S(2)}) copy-start(s32[32,1]{0,1:T(1,128)} %param.16) | copy-start | bytes 388
  57.0 380.1 %copy-start.7 = (s32[32,1]{0,1:T(1,128)S(1)}, s32[32,1]{0,1:T(1,128)}, u32[]{:S(2)}) copy-start(s32[32,1]{0,1:T(1,128)} %param.15) | copy-start | bytes 388
  57.0 380.1 %all-to-all-start = ((f32[3,2048,512]{2,0,1:T(4,128)}), f32[3,2048,512]{2,0,1:T(4,128)}, u32[]{:S(2)}, u32[]{:S(2)}) async-start(f32[3,2048,512]{2,0,1:T(4,128)} %copy.75), calls=%async_computation | async-start | bytes 33554432 | tf_op jit(solution)/shard_map/all_to_all | solution.py:74
  493.6 143.4 %all-to-all-start.1 = ((bf16[32,3,1,64,512]{4,3,1,2,0:T(8,128)(2,1)}), bf16[32,3,1,64,512]{4,3,1,2,0:T(8,128)(2,1)}, u32[]{:S(2)}, u32[]{:S(2)}) async-start(bf16[32,3,1,64,512]{4,3,1,2,0:T(8,128)(2,1)} %fusion.36), calls=%async_computation.1 | async-start | bytes 12582912 | tf_op jit(solution)/shard_map/all_to_all | solution.py:84
  528.2 9.0 %copy-start.3 = (f32[8,3,64,512]{3,0,2,1:T(8,128)S(1)}, f32[8,3,64,512]{3,0,2,1:T(8,128)}, u32[]{:S(2)}) copy-start(f32[8,3,64,512]{3,0,2,1:T(8,128)} %get-tuple-element.28) | copy-start | bytes 9437188
  531.6 9.0 %copy-start.2 = (f32[8,3,64,512]{3,0,2,1:T(8,128)S(1)}, f32[8,3,64,512]{3,0,2,1:T(8,128)}, u32[]{:S(2)}) copy-start(f32[8,3,64,512]{3,0,2,1:T(8,128)} %get-tuple-element.27) | copy-start | bytes 9437188
  637.0 6.4 copy-start.1
